TPU v7x, 32 devices: a whole 2x2x4 slice. The times are simulated.
32 devices in a mesh: grp: 2 (over y), freq: 8 (over z, x), site: 2 (over core).
Axes of the slice: x: 2, y: 2, z: 4, core: 2. Of those that a mesh axis runs over, the one named last changes fastest.
Arguments:
- green: bfloat16 [8, 1024, 8, 3, 2, 128], P('freq', None, ('grp', 'site')), parts along dimension 2, may hold values from -0.1875 to 0.1875
- slip: bfloat16 [8, 16, 8, 128], P(None, 'site'), may hold values from 0.099609375 to 1
- positions: float32 [3, 1024], replicated, may hold values from 0 to 40
- hypocenters: float32 [8, 4, 3], replicated, may hold values from 0 to 40
- slowness: float32 [8, 4], replicated, may hold values from 1 to 3
- rise: float32 [8, 16], replicated, may hold values from 0.5 to 6
- block_lists: int32 [8, 8], replicated, may hold values from 0 to 7, as said below
- block_counts: int32 [8], replicated, may hold values from 1 to 8, 48 in all
- var_counts: int32 [8], replicated, may hold values from 1 to 64, as said below
- region_map: int32 [8], replicated, may hold values from 0 to 7, each once
Outputs:
- seismograms: float32 [512, 8, 3, 2048], P('freq', ('grp', 'site')), parts along dimension 1
There are 2 independent parts, one for each index of `grp`. A program takes and returns all parts, laid end to end along the dimension named above; an argument that names none is the same for every part. Nothing has to cross between parts.
Inputs may be any that keep to these rules, and one draw needn't show every extreme that they name: `block_lists`: rupture r lists consecutive blocks s_r, s_r + 1, ... modulo 8; only its first block_counts[r] entries are used. `block_counts`: the counts sum to 48. Variations 0 .. var_counts[r] - 1 of rupture r are live. `region_map`: each row appears once.
All inputs are finite; a program needn't handle non-finite values.
Results may differ from a plain program's by a relative error of at most 0.0048.
Values may be sent and summed in bfloat16 or wider, within the bound.
A program may use at most 192 MiB of HBM per device.

v0:
```python
import math

import jax
import jax.numpy as jnp
from jax import lax
from jax.sharding import PartitionSpec as P

F = 1024
C = 3


TWO_PI = 2.0 * math.pi
OUT_GAIN = 8.0


def on_device(
    green,
    slip,
    positions,
    hypocenters,
    slowness,
    rise,
    block_lists,
    block_counts,
    var_counts,
    region_map,
):
    freq_count = lax.axis_size("freq")
    fdev_bins = green.shape[1] // freq_count
    point_count = green.shape[-1]
    rupture_count = block_lists.shape[0]
    list_len = block_lists.shape[1]
    hypo_count = hypocenters.shape[1]
    wave_len = 2 * F
    slip_all = lax.all_gather(slip, "site", axis=1, tiled=True)
    real_count = slip_all.shape[1]
    first_bin = lax.axis_index("freq") * fdev_bins
    local_bins = first_bin + jnp.arange(fdev_bins, dtype=jnp.int32)
    omegas = TWO_PI * local_bins.astype(jnp.float32) / wave_len
    points_all = positions.reshape(3, positions.shape[1] // point_count, point_count)
    slot_total = rupture_count * list_len
    slot_index = jnp.arange(slot_total, dtype=jnp.int32)
    slot_rup = slot_index // list_len
    slot_pos = slot_index % list_len
    slot_live = slot_pos < block_counts[slot_rup]
    group_size = math.gcd(slot_total, 32)
    turn_count = slot_total // group_size
    rupture_ids = jnp.arange(rupture_count, dtype=jnp.int32)
    tiles_here = lax.all_to_all(green, "freq", split_axis=1, concat_axis=0, tiled=True)
    site_items = tiles_here.shape[2]

    def one_turn(turn_index, totals):
        start = turn_index * group_size
        group_rup = lax.dynamic_slice_in_dim(slot_rup, start, group_size)
        group_pos = lax.dynamic_slice_in_dim(slot_pos, start, group_size)
        group_live = lax.dynamic_slice_in_dim(slot_live, start, group_size)
        blocks = block_lists[group_rup, group_pos]
        tile = tiles_here[region_map[blocks]].astype(jnp.float32)
        points = points_all[:, blocks, :].transpose(1, 0, 2)
        centers = hypocenters[group_rup]
        slows = slowness[group_rup]
        sq_dist = jnp.sum((points[:, None, :, :] - centers[:, :, :, None]) ** 2, axis=2)
        onset_time = slows[:, :, None] * jnp.sqrt(sq_dist)
        phases = omegas[None, None, :, None] * onset_time[:, :, None, :]
        wave_re = jnp.cos(phases)[:, :, :, None, None, :]
        wave_im = -jnp.sin(phases)[:, :, :, None, None, :]
        tile_re = tile[:, None, :, :, :, 0, :]
        tile_im = tile[:, None, :, :, :, 1, :]
        weighted = jnp.stack(
            [wave_re * tile_re - wave_im * tile_im, wave_re * tile_im + wave_im * tile_re], axis=5
        ).astype(jnp.bfloat16)
        amps = slip_all[group_rup, :, group_pos]
        amps = jnp.where(group_live[:, None, None], amps, jnp.zeros_like(amps))
        onehot = (group_rup[None, :] == rupture_ids[:, None]).astype(jnp.bfloat16)
        routed = onehot[:, :, None, None] * amps[None, :, :, :]
        term = jnp.einsum(
            "rgkp,ghfscqp->rkhfscq", routed, weighted, preferred_element_type=jnp.float32
        )
        return totals + term

    start_totals = jnp.zeros(
        (rupture_count, real_count, hypo_count, fdev_bins, site_items, C, 2), jnp.float32
    )
    totals = lax.fori_loop(0, turn_count, one_turn, start_totals)
    ratio = omegas[None, None, :] * rise[:, :, None]
    denom = 1.0 + ratio * ratio
    stf_re = (1.0 / denom)[:, :, None, :, None, None]
    stf_im = (-ratio / denom)[:, :, None, :, None, None]
    part_re = totals[..., 0]
    part_im = totals[..., 1]
    spec_re = stf_re * part_re - stf_im * part_im
    spec_im = stf_re * part_im + stf_im * part_re
    spectrum = jnp.stack([spec_re, spec_im], axis=-1).transpose(0, 1, 2, 4, 5, 6, 3)
    variation = (
        jnp.arange(real_count, dtype=jnp.int32)[:, None] * hypo_count
        + jnp.arange(hypo_count, dtype=jnp.int32)[None, :]
    )
    live = variation[None, :, :] < var_counts[:, None, None]
    spectrum = jnp.where(live[:, :, :, None, None, None, None], spectrum, jnp.zeros_like(spectrum))
    spectrum = spectrum.reshape(
        rupture_count * real_count * hypo_count, site_items, C, 2, fdev_bins
    ).astype(jnp.bfloat16)
    own_rows = lax.all_to_all(spectrum, "freq", split_axis=0, concat_axis=4, tiled=True)
    row_count = own_rows.shape[0]
    site_count = own_rows.shape[1]
    spec_rows = own_rows.reshape(row_count * site_count * C, 2 * F)
    bins = jnp.arange(F, dtype=jnp.int32)
    piece_len = min(512, wave_len)
    pieces = []
    for piece_index in range(wave_len // piece_len):
        samples = piece_index * piece_len + jnp.arange(piece_len, dtype=jnp.int32)
        products = bins[:, None] * samples[None, :] % wave_len
        angles = TWO_PI * products.astype(jnp.float32) / wave_len
        wave_table = jnp.concatenate([jnp.cos(angles), -jnp.sin(angles)], axis=0).astype(
            jnp.bfloat16
        )
        pieces.append(
            jnp.dot(spec_rows, wave_table, preferred_element_type=jnp.float32)
            * (OUT_GAIN / math.sqrt(F))
        )
    motion = jnp.concatenate(pieces, axis=1)
    return motion.reshape(row_count, site_count, C, wave_len)


def solution(mesh):
    placed = (
        P("freq", None, ("grp", "site"), None, None, None),
        P(None, "site", None, None),
        P(),
        P(),
        P(),
        P(),
        P(),
        P(),
        P(),
        P(),
    )
    return jax.shard_map(
        on_device,
        mesh=mesh,
        in_specs=placed,
        out_specs=P("freq", ("grp", "site"), None, None),
        check_vma=False,
    )
```

profile of v0, /device:TPU:0, one launch (start us, length us, event | category | flops | bytes accessed | tf_op | source)
XLA Modules:
  0.0 425.5 jit_solution(9974423023385828386)
XLA Ops:
  0.0 7.4 %all-to-all-start = ((bf16[1,1024,2,3,2,128]{5,4,3,2,0,1:T(2,128)(2,1)}), bf16[1,1024,2,3,2,128]{5,4,3,2,0,1:T(2,128)(2,1)S(1)}, u32[]{:S(2)}, u32[]{:S(2)}) async-start(bf16[1,1024,2,3,2,128]{5,4,3,2,0,1:T(2,128)(2,1)} %bitcast.80), calls=%async_computation | async-start | bytes 6291456 | tf_op jit(solution)/shard_map/all_to_all | solution.py:49
  7.7 2.1 all_gather.3
  9.9 0.7 fusion.80
  10.6 5.2 %fusion.75 = pred[64]{0:T(512)(128)(4,1)S(1)} fusion(s32[]{:T(128)} %bitcast.2, s32[]{:T(128)} %bitcast.3, s32[]{:T(128)} %bitcast.4, s32[]{:T(128)} %bitcast.5, s32[]{:T(128)} %bitcast.6, s32[]{:T(128)} %bitcast.8, s32[]{:T(128)} %bitcast.7, s32[]{:T(128)} %bitcast.1), kind=kLoop, calls=%fused_computation.141 | loop fusion | flops 2048 | bytes 96 | tf_op jit(solution)/shard_map/lt | solution.py:45
  15.8 0.7 broadcast_compare_fusion
  16.4 0.7 fusion.73
  17.2 61.0 %all-to-all-done = bf16[1,1024,2,3,2,128]{5,4,3,2,0,1:T(2,128)(2,1)S(1)} async-done(((bf16[1,1024,2,3,2,128]{5,4,3,2,0,1:T(2,128)(2,1)}), bf16[1,1024,2,3,2,128]{5,4,3,2,0,1:T(2,128)(2,1)S(1)}, u32[]{:S(2)}, u32[]{:S(2)}) %all-to-all-start) | async-done | bytes 3145760 | tf_op jit(solution)/shard_map/all_to_all | solution.py:49
  78.2 1.6 copy-done.2
  79.8 2.8 copy.71
  82.7 274.8 %while.14 = (s32[]{:T(128)}, f32[8,16,4,128,2,3,2]{3,1,6,5,4,2,0:T(8,128)}, s32[64]{0:T(128)S(1)}, pred[64]{0:T(512)(128)(4,1)S(1)}, s32[64]{0:T(128)S(1)}, /*in...) while((s32[]{:T(128)}, ...), condition=%wide.region_2.3_spmd.clone, body=%wide.region_0.2_spmd.clone.sunk | while | flops 6658150912 | bytes 280112832 | solution.py:84
  82.8 0.7 gather_fusion.1
  83.5 0.6 gather_fusion.2
  84.2 0.6 gather_fusion
  85.8 32.0 %multiply_cosine_fusion.2 = (f32[32,4,128,128]{3,2,0,1:T(8,128)}, f32[32,4,128,128]{3,2,0,1:T(8,128)}) fusion(f32[32,4,128]{2,0,1:T(8,128)S(1)} %sqrt_multiply_fusion.2, f32[128]{0:T(128)S(1)} %convert_multiply_fusion.3), kind=kLoop, calls=%fused_computation.16.clone.1 | loop fusion | flops 4194304 | bytes 16843264 | tf_op jit(solution)/shard_map/while/body/eval_jaxpr/cos | solution.py:65
  117.7 0.7 gather_fusion.4
  118.5 6.8 %gather_fusion.5 = bf16[32,128,2,3,2,128]{5,1,4,3,2,0:T(8,128)(2,1)} fusion(bf16[8,128,2,3,2,128]{5,1,4,3,2,0:T(8,128)(2,1)S(1)} %get-tuple-element.556, s32[1024]{0:T(1024)S(1)} %pad_clamp_fusion.8), kind=kCustom, calls=%fused_computation.6.clone.clone.1 | custom fusion | bytes 25165952 | tf_op jit(solution)/shard_map/while/body/eval_jaxpr/gather | solution.py:58
  125.3 14.4 %convert_element_type.116 = f32[32,128,2,3,2,128]{5,1,4,3,2,0:T(8,128)} convert(bf16[32,128,2,3,2,128]{5,1,4,3,2,0:T(8,128)(2,1)} %gather_fusion.5) | non-fusion elementwise | flops 6291456 | bytes 37748736 | tf_op jit(solution)/shard_map/while/body/eval_jaxpr/convert_element_type | solution.py:58
  139.7 14.2 %slice_bitcast_fusion.3 = (f32[32,128,2,3,128]{4,1,3,2,0:T(8,128)S(1)}, f32[32,128,2,3,128]{4,1,3,2,0:T(8,128)}) fusion(f32[32,128,2,3,2,128]{5,1,4,3,2,0:T(8,128)} %convert_element_type.116), kind=kLoop, calls=%fused_computation.14.clone.1 | loop fusion | bytes 50331648 | tf_op jit(solution)/shard_map/while/body/eval_jaxpr/mul | solution.py:70
  153.9 41.2 %subtract_convert_fusion.2 = (bf16[32,4,128,2,3,1,128]{6,2,0,5,4,3,1:T(8,128)(2,1)}, bf16[32,4,128,2,3,1,128]{6,2,0,5,4,3,1:T(8,128)(2,1)}) fusion(f32[32,4,128,128]{3,2,0,1:T(8,128)} %get-tuple-element.505, f32[32,4,128,128]{3,2,0,1:T(8,128)} %get-tuple-element.506, f32[32,128,2,3,128]{4,1,3,2,0:T(8,128)S(1)} %get-tuple-element.507, ...), kind=kLoop, calls=%fused_computation.11.clone.1 | loop fusion | flops 100663296 | bytes 92274688 | tf_op jit(solution)/shard_map/convert
  195.1 1.6 gather_fusion.6
  196.9 23.2 %bitcast_add_fusion.2 = f32[8,16,4,128,2,3,2]{3,1,6,5,4,2,0:T(8,128)} fusion(f32[8,16,4,128,2,3,2]{3,1,6,5,4,2,0:T(8,128)} %get-tuple-element.529, bf16[32,4,128,2,3,1,128]{6,2,0,5,4,3,1:T(8,128)(2,1)} %get-tuple-element.509, bf16[32,4,128,2,3,1,128]{6,2,0,5,4,3,1:T(8,128)(2,1)} %get-tuple-element.510, pred[]{:T(512)S(6)} %compare.103, ...), kind=kOutput, calls=%fused_computation.18.clone.1 | convolution fusion | flops 6546784256 | bytes 56754688 | tf_op jit(solution)/shard_map/while/body/eval_jaxpr/rgkp,ghfscqp->rkhfscq/dot_general | solution.py:76
  220.2 0.7 gather_fusion.1
  220.9 0.6 gather_fusion.2
  221.5 0.6 gather_fusion
  223.1 32.0 %multiply_cosine_fusion.2 = (f32[32,4,128,128]{3,2,0,1:T(8,128)}, f32[32,4,128,128]{3,2,0,1:T(8,128)}) fusion(f32[32,4,128]{2,0,1:T(8,128)S(1)} %sqrt_multiply_fusion.2, f32[128]{0:T(128)S(1)} %convert_multiply_fusion.3), kind=kLoop, calls=%fused_computation.16.clone.1 | loop fusion | flops 4194304 | bytes 16843264 | tf_op jit(solution)/shard_map/while/body/eval_jaxpr/cos | solution.py:65
  255.1 0.7 gather_fusion.4
  255.8 6.6 %gather_fusion.5 = bf16[32,128,2,3,2,128]{5,1,4,3,2,0:T(8,128)(2,1)} fusion(bf16[8,128,2,3,2,128]{5,1,4,3,2,0:T(8,128)(2,1)S(1)} %get-tuple-element.556, s32[1024]{0:T(1024)S(1)} %pad_clamp_fusion.8), kind=kCustom, calls=%fused_computation.6.clone.clone.1 | custom fusion | bytes 25165952 | tf_op jit(solution)/shard_map/while/body/eval_jaxpr/gather | solution.py:58
  262.4 14.4 %convert_element_type.116 = f32[32,128,2,3,2,128]{5,1,4,3,2,0:T(8,128)} convert(bf16[32,128,2,3,2,128]{5,1,4,3,2,0:T(8,128)(2,1)} %gather_fusion.5) | non-fusion elementwise | flops 6291456 | bytes 37748736 | tf_op jit(solution)/shard_map/while/body/eval_jaxpr/convert_element_type | solution.py:58
  276.8 14.2 %slice_bitcast_fusion.3 = (f32[32,128,2,3,128]{4,1,3,2,0:T(8,128)S(1)}, f32[32,128,2,3,128]{4,1,3,2,0:T(8,128)}) fusion(f32[32,128,2,3,2,128]{5,1,4,3,2,0:T(8,128)} %convert_element_type.116), kind=kLoop, calls=%fused_computation.14.clone.1 | loop fusion | bytes 50331648 | tf_op jit(solution)/shard_map/while/body/eval_jaxpr/mul | solution.py:70
  291.0 41.2 %subtract_convert_fusion.2 = (bf16[32,4,128,2,3,1,128]{6,2,0,5,4,3,1:T(8,128)(2,1)}, bf16[32,4,128,2,3,1,128]{6,2,0,5,4,3,1:T(8,128)(2,1)}) fusion(f32[32,4,128,128]{3,2,0,1:T(8,128)} %get-tuple-element.505, f32[32,4,128,128]{3,2,0,1:T(8,128)} %get-tuple-element.506, f32[32,128,2,3,128]{4,1,3,2,0:T(8,128)S(1)} %get-tuple-element.507, ...), kind=kLoop, calls=%fused_computation.11.clone.1 | loop fusion | flops 100663296 | bytes 92274688 | tf_op jit(solution)/shard_map/convert
  332.2 1.6 gather_fusion.6
  334.0 23.5 %bitcast_add_fusion.2 = f32[8,16,4,128,2,3,2]{3,1,6,5,4,2,0:T(8,128)} fusion(f32[8,16,4,128,2,3,2]{3,1,6,5,4,2,0:T(8,128)} %get-tuple-element.529, bf16[32,4,128,2,3,1,128]{6,2,0,5,4,3,1:T(8,128)(2,1)} %get-tuple-element.509, bf16[32,4,128,2,3,1,128]{6,2,0,5,4,3,1:T(8,128)(2,1)} %get-tuple-element.510, pred[]{:T(512)S(6)} %compare.103, ...), kind=kOutput, calls=%fused_computation.18.clone.1 | convolution fusion | flops 6546784256 | bytes 56754688 | tf_op jit(solution)/shard_map/while/body/eval_jaxpr/rgkp,ghfscqp->rkhfscq/dot_general | solution.py:76
  357.5 2.4 multiply_subtract_fusion
  360.3 2.0 copy.72
  362.3 2.8 copy.73
  365.1 3.6 all-to-all-start.1
  368.7 9.3 %negate_convert_fusion.3 = (bf16[1024,512]{1,0:T(8,128)(2,1)}, bf16[1024,512]{1,0:T(8,128)(2,1)}) fusion(), kind=kLoop, calls=%fused_computation.97 | loop fusion | flops 8912896 | bytes 2097152 | tf_op jit(solution)/shard_map/convert.9
  378.0 9.4 %cosine_convert_fusion.1 = (bf16[1024,512]{1,0:T(8,128)(2,1)}, bf16[1024,512]{1,0:T(8,128)(2,1)}) fusion(s32[512]{0:T(512)S(1)} %iota_add_fusion.1), kind=kLoop, calls=%fused_computation.90 | loop fusion | flops 8912896 | bytes 2099200 | tf_op jit(solution)/shard_map/convert.4
  387.4 9.4 %cosine_convert_fusion.2 = (bf16[1024,512]{1,0:T(8,128)(2,1)}, bf16[1024,512]{1,0:T(8,128)(2,1)}) fusion(s32[512]{0:T(512)S(1)} %iota_add_fusion.2), kind=kLoop, calls=%fused_computation.94 | loop fusion | flops 8912896 | bytes 2099200 | tf_op jit(solution)/shard_map/convert.6
  396.8 9.3 %cosine_convert_fusion = (bf16[1024,512]{1,0:T(8,128)(2,1)}, bf16[1024,512]{1,0:T(8,128)(2,1)}) fusion(s32[512]{0:T(512)S(1)} %iota_add_fusion), kind=kLoop, calls=%fused_computation.86 | loop fusion | flops 8912896 | bytes 2099200 | tf_op jit(solution)/shard_map/convert.2
  406.1 1.8 copy.85
  407.9 0.7 reshape.209
  408.7 2.7 fusion.62
  411.4 1.0 fusion.65
  412.9 1.0 fusion.68
  414.5 1.0 fusion.59
  415.7 3.0 reshape.210
  418.7 6.8 %copy.75 = f32[64,2,3,2048]{3,1,2,0:T(2,128)} copy(f32[64,2,3,2048]{3,2,1,0:T(4,128)} %reshape.210) | data formatting | bytes 6291456 | tf_op jit(solution)/shard_map/reshape | solution.py:122
  (81 shorter events, 4.7 us)
Async XLA Ops:
  0.0 7.5 %copy-start.10 = (bf16[8,8,8,128]{3,2,1,0:T(8,128)(2,1)S(1)}, bf16[8,8,8,128]{3,2,1,0:T(8,128)(2,1)}, u32[]{:S(2)}) copy-start(bf16[8,8,8,128]{3,2,1,0:T(8,128)(2,1)} %param.13) | copy-start | bytes 393220
  0.0 7.5 %copy-start.13 = (f32[8,4,3]{0,1,2:T(4,128)S(1)}, f32[8,4,3]{0,1,2:T(4,128)}, u32[]{:S(2)}) copy-start(f32[8,4,3]{0,1,2:T(4,128)} %param.15) | copy-start | bytes 1156
  0.0 7.6 %copy-start.15 = (f32[8,4]{0,1:T(4,128)S(1)}, f32[8,4]{0,1:T(4,128)}, u32[]{:S(2)}) copy-start(f32[8,4]{0,1:T(4,128)} %param.16) | copy-start | bytes 388
  0.0 9.8 %copy-start.11 = (s32[8]{0:T(128)S(1)}, s32[8]{0:T(128)}, u32[]{:S(2)}) copy-start(s32[8]{0:T(128)} %param.19) | copy-start | bytes 100
  0.0 15.7 %copy-start.16 = (s32[8]{0:T(128)S(1)}, s32[8]{0:T(128)}, u32[]{:S(2)}) copy-start(s32[8]{0:T(128)} %param.20) | copy-start | bytes 100
  0.0 16.4 %copy-start.14 = (f32[8,16]{1,0:T(8,128)S(1)}, f32[8,16]{1,0:T(8,128)}, u32[]{:S(2)}) copy-start(f32[8,16]{1,0:T(8,128)} %param.17) | copy-start | bytes 1540
  0.0 78.1 %all-to-all-start = ((bf16[1,1024,2,3,2,128]{5,4,3,2,0,1:T(2,128)(2,1)}), bf16[1,1024,2,3,2,128]{5,4,3,2,0,1:T(2,128)(2,1)S(1)}, u32[]{:S(2)}, u32[]{:S(2)}) async-start(bf16[1,1024,2,3,2,128]{5,4,3,2,0,1:T(2,128)(2,1)} %bitcast.80), calls=%async_computation | async-start | bytes 6291456 | tf_op jit(solution)/shard_map/all_to_all | solution.py:49
  78.2 1.6 copy-start.2
  79.8 2.8 copy-start
  79.8 2.8 copy-start.1
  79.8 2.8 copy-start.3
  357.5 2.4 copy-start.12
  365.1 41.1 %all-to-all-start.1 = ((bf16[512,2,3,2,128]{4,3,2,1,0:T(2,128)(2,1)}), bf16[512,2,3,2,128]{4,3,2,1,0:T(2,128)(2,1)S(1)}, u32[]{:S(2)}, u32[]{:S(2)}) async-start(bf16[512,2,3,2,128]{4,3,2,1,0:T(2,128)(2,1)} %copy.73), calls=%async_computation.1 | async-start | bytes 3145728 | tf_op jit(solution)/shard_map/all_to_all | solution.py:103
  408.7 2.7 copy-start.6
  408.7 2.7 copy-start.7
  411.4 1.2 copy-start.8
  411.4 1.5 copy-start.9
  412.9 1.2 copy-start.4
  412.9 1.5 copy-start.5
where the time goes:
time: 426 us; the launch traced here: 425 us
  other arithmetic  223 us (52%)
  local copies, waits for them, and re-layouts  75.5 us (18%)
  waiting for transfers between devices  61 us (14%)
  matrix products  52.3 us (12%)
  starting transfers between devices  11.1 us (3%)
    another operation x6, other arithmetic  120 us
    cos x2, other arithmetic, one_turn(): wave_re = jnp.cos(phases)[:, :, :, None, None, :]  63.9 us
    all_to_all x1, waiting for transfers between devices, on_device(): lax.all_to_all(green, 'freq', split_axis=1, concat_axis=0, tiled=True)  61 us
    dot_general x2, matrix products, one_turn(): jnp.einsum('rgkp,ghfscqp->rkhfscq', routed, weighted, preferred_element_t...  46.6 us
    convert_element_type x2, other arithmetic, one_turn(): tile = tiles_here[region_map[blocks]].astype(jnp.float32)  28.8 us
    mul x2, local copies, waits for them, and re-layouts, one_turn(): wave_re * tile_re - wave_im * tile_im  28.4 us
    gather x4, local copies, waits for them, and re-layouts, one_turn(): tile = tiles_here[region_map[blocks]].astype(jnp.float32)  14.8 us
    reshape x2, local copies, waits for them, and re-layouts, on_device(): return motion.reshape(row_count, site_count, C, wave_len)  9.76 us
  transfers between devices with their start and end apart: 2, of which 1 were waited for; matrix products, arithmetic and copies ran while one was open for 11% of the time, Pallas kernels for 0%

commit v1 on v0

--- a/solution.py
+++ b/solution.py
@@ -3,6 +3,8 @@
 import jax
 import jax.numpy as jnp
 from jax import lax
+from jax.experimental import pallas as pl
+from jax.experimental.pallas import tpu as pltpu
 from jax.sharding import PartitionSpec as P
 
 F = 1024
@@ -11,9 +13,250 @@
 
 TWO_PI = 2.0 * math.pi
 OUT_GAIN = 8.0
+LANES = 128
+
+SIN_COEFS = tuple((-1) ** i * math.pi ** (2 * i + 1) / math.factorial(2 * i + 1) for i in range(7))
+COS_COEFS = tuple((-1) ** i * math.pi ** (2 * i) / math.factorial(2 * i) for i in range(7))
+
+
+def turn_waves(turns):
+    frac = turns - jnp.round(turns)
+    square = frac * frac
+    half_sin = SIN_COEFS[-1]
+    for coef in SIN_COEFS[-2::-1]:
+        half_sin = half_sin * square + coef
+    half_sin = half_sin * frac
+    half_cos = COS_COEFS[-1]
+    for coef in COS_COEFS[-2::-1]:
+        half_cos = half_cos * square + coef
+    return 1.0 - 2.0 * half_sin * half_sin, 2.0 * half_sin * half_cos
+
+
+def synth_kernel(
+    lists,
+    counts,
+    var_counts,
+    regions,
+    first_bin,
+    centers,
+    slows,
+    tiles,
+    slip,
+    points,
+    rise,
+    out,
+    cos_buf,
+    sin_buf,
+    total,
+):
+    rup = pl.program_id(0)
+    sites, bins = tiles.shape[1], tiles.shape[4]
+    real_count = slip.shape[1]
+    list_len = slip.shape[0] // pl.num_programs(0)
+    hypo_count = cos_buf.shape[0] * 2
+    step = 16
+    start = first_bin[0]
+    total[...] = jnp.zeros_like(total)
+
+    def one_slot(place, carry):
+        block = lists[rup * list_len + place]
+        region = regions[block]
+        xyz = points[block]
+        low = lax.broadcasted_iota(jnp.int32, (step, LANES), 0).astype(jnp.float32)
+        high = (start + step * lax.broadcasted_iota(jnp.int32, (bins // step, LANES), 0)).astype(
+            jnp.float32
+        )
+        for hypo in range(hypo_count):
+            at = (rup * hypo_count + hypo) * 3
+            sq_dist = jnp.zeros((1, LANES), jnp.float32)
+            for axis in range(3):
+                gap = xyz[axis : axis + 1, :] - centers[at + axis]
+                sq_dist = sq_dist + gap * gap
+            onset = slows[rup * hypo_count + hypo] * jnp.sqrt(sq_dist)
+            rate = onset * (1.0 / (2 * F))
+            low_cos, low_sin = turn_waves(low * rate)
+            high_cos, high_sin = turn_waves(high * rate)
+            lane = (hypo % 2) * LANES
+            for part in range(bins // step):
+                hc, hs = high_cos[part : part + 1], high_sin[part : part + 1]
+                cos = (hc * low_cos - hs * low_sin).astype(jnp.bfloat16)
+                sin = (hs * low_cos + hc * low_sin).astype(jnp.bfloat16)
+                rows = pl.ds(part * step, step)
+                cos_buf[hypo // 2, rows, lane : lane + LANES] = cos
+                sin_buf[hypo // 2, rows, lane : lane + LANES] = sin
+        amps = slip[rup * list_len + place]
+        none = jnp.zeros_like(amps)
+        paired = jnp.concatenate(
+            [jnp.concatenate([amps, none], axis=1), jnp.concatenate([none, amps], axis=1)], axis=0
+        )
+        for site in range(sites):
+            for comp in range(C):
+                tile_re = tiles[region, site, comp, 0]
+                tile_im = tiles[region, site, comp, 1]
+                tile_re = jnp.concatenate([tile_re, tile_re], axis=1)
+                tile_im = jnp.concatenate([tile_im, tile_im], axis=1)
+                for pair in range(hypo_count // 2):
+                    cos, sin = cos_buf[pair], sin_buf[pair]
+                    weighted = jnp.concatenate(
+                        [cos * tile_re + sin * tile_im, cos * tile_im - sin * tile_re], axis=0
+                    )
+                    total[site, comp, pair] += lax.dot_general(
+                        paired,
+                        weighted,
+                        (((1,), (1,)), ((), ())),
+                        preferred_element_type=jnp.float32,
+                    )
+        return carry
+
+    lax.fori_loop(0, counts[rup], one_slot, 0)
+    omegas = (start + lax.broadcasted_iota(jnp.int32, (real_count, bins), 1)).astype(
+        jnp.float32
+    ) * (TWO_PI / (2 * F))
+    ratio = omegas * rise[0]
+    stf_re = 1.0 / (1.0 + ratio * ratio)
+    stf_im = -ratio * stf_re
+    reals = lax.broadcasted_iota(jnp.int32, (real_count, bins), 0)
+    for pair in range(hypo_count // 2):
+        for side in range(2):
+            hypo = pair * 2 + side
+            live = reals * hypo_count + hypo < var_counts[rup]
+            rows = slice(side * real_count, (side + 1) * real_count)
+            kept = slice(hypo * real_count, (hypo + 1) * real_count)
+            for site in range(sites):
+                for comp in range(C):
+                    part_re = total[site, comp, pair, rows, :bins]
+                    part_im = total[site, comp, pair, rows, bins:]
+                    spec_re = stf_re * part_re - stf_im * part_im
+                    spec_im = stf_re * part_im + stf_im * part_re
+                    out[0, site, comp, 0, kept] = jnp.where(live, spec_re, 0.0).astype(out.dtype)
+                    out[0, site, comp, 1, kept] = jnp.where(live, spec_im, 0.0).astype(out.dtype)
+
+
+def synthesize(tiles, slip, points, rise, scalars, hypo_count):
+    rupture_count = rise.shape[0]
+    real_count = rise.shape[1]
+    _, sites, _, _, bins, _ = tiles.shape
+    whole = pl.BlockSpec(memory_space=pltpu.VMEM)
+    return pl.pallas_call(
+        synth_kernel,
+        grid_spec=pltpu.PrefetchScalarGridSpec(
+            num_scalar_prefetch=len(scalars),
+            grid=(rupture_count,),
+            in_specs=[
+                whole,
+                whole,
+                whole,
+                pl.BlockSpec((1, real_count, bins), lambda r, *_: (r, 0, 0)),
+            ],
+            out_specs=pl.BlockSpec(
+                (1, sites, C, 2, hypo_count * real_count, bins),
+                lambda r, *_: (r, 0, 0, 0, 0, 0),
+            ),
+            scratch_shapes=[
+                pltpu.VMEM((hypo_count // 2, bins, 2 * LANES), jnp.bfloat16),
+                pltpu.VMEM((hypo_count // 2, bins, 2 * LANES), jnp.bfloat16),
+                pltpu.VMEM((sites, C, hypo_count // 2, 2 * real_count, 2 * bins), jnp.float32),
+            ],
+        ),
+        out_shape=jax.ShapeDtypeStruct(
+            (rupture_count, sites, C, 2, hypo_count * real_count, bins), jnp.bfloat16
+        ),
+        compiler_params=pltpu.CompilerParams(dimension_semantics=("arbitrary",)),
+        cost_estimate=pl.CostEstimate(
+            flops=sites * 2 * 10**10, bytes_accessed=4 * 10**7, transcendentals=0
+        ),
+    )(*scalars, tiles, slip, points, rise)
+
+
+def make_wave_table():
+    wave_len = 2 * F
+    chunk = LANES
+    bins = jnp.arange(F, dtype=jnp.int32)[:, None]
+
+    def waves(samples):
+        angles = TWO_PI / wave_len * (bins * samples[None, :] % wave_len).astype(jnp.float32)
+        return jnp.cos(angles), jnp.sin(angles)
+
+    low_cos, low_sin = waves(jnp.arange(chunk, dtype=jnp.int32))
+    high_cos, high_sin = waves(jnp.arange(wave_len // chunk, dtype=jnp.int32) * chunk)
+    low_cos, low_sin = low_cos[:, None, :], low_sin[:, None, :]
+    high_cos, high_sin = high_cos[:, :, None], high_sin[:, :, None]
+    cos = (high_cos * low_cos - high_sin * low_sin).astype(jnp.bfloat16)
+    sin = (high_sin * low_cos + high_cos * low_sin).astype(jnp.bfloat16)
+    return jnp.stack([cos, -sin]).reshape(2 * F, wave_len)
 
 
 def on_device(
+    green,
+    slip,
+    positions,
+    hypocenters,
+    slowness,
+    rise,
+    block_lists,
+    block_counts,
+    var_counts,
+    region_map,
+):
+    freq_count = lax.axis_size("freq")
+    site_shards = lax.axis_size("site")
+    fdev_bins = green.shape[1] // freq_count
+    point_count = green.shape[-1]
+    rupture_count, list_len = block_lists.shape
+    hypo_count = hypocenters.shape[1]
+    wave_len = 2 * F
+    block_total = positions.shape[1] // point_count
+    pieces = [slip]
+    for shift in range(1, site_shards):
+        pieces.append(
+            lax.ppermute(
+                slip, "site", [(i, (i - shift) % site_shards) for i in range(site_shards)]
+            )
+        )
+    ring = jnp.stack(pieces)
+    own = lax.axis_index("site")
+    order = (jnp.arange(site_shards) - own) % site_shards
+    slip_all = ring[order].transpose(1, 3, 0, 2, 4)
+    real_count = site_shards * slip.shape[1]
+    slip_all = slip_all.reshape(rupture_count * list_len, real_count, point_count)
+    points = positions.reshape(3, block_total, point_count).transpose(1, 0, 2)
+    first_bin = (lax.axis_index("freq") * fdev_bins).astype(jnp.int32).reshape(1)
+    scalars = (
+        block_lists.reshape(-1),
+        block_counts,
+        var_counts,
+        region_map,
+        first_bin,
+        hypocenters.reshape(-1),
+        slowness.reshape(-1),
+    )
+    rise_rows = jnp.broadcast_to(rise[:, :, None], (rupture_count, real_count, fdev_bins))
+    site_items = green.shape[2]
+    rows_here, _, _, comps, _, _ = green.shape
+    wave_table = make_wave_table()
+    motions = []
+    for site in range(site_items):
+        piece = green[:, :, site : site + 1].reshape(
+            rows_here, freq_count, fdev_bins, 1, comps, 2, point_count
+        )
+        piece = piece.transpose(1, 0, 3, 4, 5, 2, 6)
+        tiles = lax.all_to_all(piece, "freq", split_axis=0, concat_axis=0, tiled=True)
+        tiles = tiles.reshape(freq_count * rows_here, 1, comps, 2, fdev_bins, point_count)
+        spectrum = synthesize(tiles, slip_all, points, rise_rows, scalars, hypo_count)
+        own_rows = lax.all_to_all(spectrum, "freq", split_axis=0, concat_axis=0, tiled=True)
+        own_rows = own_rows.reshape(
+            freq_count, rupture_count // freq_count, comps, 2, hypo_count, real_count, fdev_bins
+        ).transpose(1, 5, 4, 2, 3, 0, 6)
+        row_count = rupture_count // freq_count * hypo_count * real_count
+        spec_rows = own_rows.reshape(row_count * comps, wave_len)
+        motion = jnp.dot(spec_rows, wave_table, preferred_element_type=jnp.float32) * (
+            OUT_GAIN / math.sqrt(F)
+        )
+        motions.append(motion.reshape(row_count, 1, comps, wave_len))
+    return jnp.concatenate(motions, axis=1)
+
+
+def on_device_small(
     green,
     slip,
     positions,
@@ -122,6 +365,16 @@
     return motion.reshape(row_count, site_count, C, wave_len)
 
 
+def on_device_any(green, slip, positions, hypocenters, *rest):
+    freq_count = lax.axis_size("freq")
+    fdev_bins = green.shape[1] // freq_count
+    rupture_count, hypo_count = hypocenters.shape[:2]
+    lanes_fit = fdev_bins == LANES and green.shape[-1] == LANES
+    if lanes_fit and hypo_count % 2 == 0 and rupture_count % freq_count == 0:
+        return on_device(green, slip, positions, hypocenters, *rest)
+    return on_device_small(green, slip, positions, hypocenters, *rest)
+
+
 def solution(mesh):
     placed = (
         P("freq", None, ("grp", "site"), None, None, None),
@@ -136,7 +389,7 @@
         P(),
     )
     return jax.shard_map(
-        on_device,
+        on_device_any,
         mesh=mesh,
         in_specs=placed,
         out_specs=P("freq", ("grp", "site"), None, None),

time: 426 us -> 183 us (0.43)
  other arithmetic: 223 us -> 30.1 us
  Pallas kernels: 0 us -> 56.3 us
  local copies, waits for them, and re-layouts: 75.5 us -> 26.7 us
  matrix products: 52.3 us -> 13.1 us
  waiting for transfers between devices: 61 us -> 32.7 us
  starting transfers between devices: 11.1 us -> 23.5 us
    another operation x6 -> x2, other arithmetic: 120 us -> 6.29 us  [the longest x1 6.26 us: make_wave_table(): return jnp.stack([cos, -sin]).reshape(2 * F, wave_len)]
    cos x2 -> x1, other arithmetic: 63.9 us -> 0.34 us  [waves(): return (jnp.cos(angles), jnp.sin(angles))]
    pallas_call x0 -> x2, Pallas kernels: none -> 56.3 us  [synthesize(): pl.pallas_call(synth_kernel, grid_spec=pltpu.PrefetchScalarGridSpec(num_s...]
    dot_general x2 -> x0, matrix products: 46.6 us -> none  [one_turn(): jnp.einsum('rgkp,ghfscqp->rkhfscq', routed, weighted, preferred_element_t...]
    mul x2 -> x0, local copies, waits for them, and re-layouts: 28.4 us -> none  [one_turn(): wave_re * tile_re - wave_im * tile_im]
    all_to_all x2 -> x4, waiting for transfers between devices: 61 us -> 32.7 us  [the longest x2 32.7 us: on_device(): lax.all_to_all(piece, 'freq', split_axis=0, concat_axis=0, tiled=True)]
    gather x21 -> x1, local copies, waits for them, and re-layouts: 24 us -> 0.6 us  [on_device(): slip_all = ring[order].transpose(1, 3, 0, 2, 4)]
    convert_element_type x5 -> x1, other arithmetic: 29.2 us -> 9.37 us  [make_wave_table(): cos = (high_cos * low_cos - high_sin * low_sin).astype(jnp.bfloat16)]
  transfers between devices with their start and end apart: 2 -> 5, of which waited for: 1 -> 1; matrix products, arithmetic and copies ran while one was open for 11% -> 24% of each run, Pallas kernels for 0% -> 31%
where the time goes in v1:
time: 183 us
  Pallas kernels  56.3 us (31%)
  waiting for transfers between devices  32.7 us (18%)
  other arithmetic  30.1 us (16%)
  local copies, waits for them, and re-layouts  26.7 us (15%)
  starting transfers between devices  23.5 us (13%)
  matrix products  13.1 us (7%)
    pallas_call x2, Pallas kernels, synthesize(): pl.pallas_call(synth_kernel, grid_spec=pltpu.PrefetchScalarGridSpec(num_s...  56.3 us
    all_to_all x2, waiting for transfers between devices, on_device(): lax.all_to_all(piece, 'freq', split_axis=0, concat_axis=0, tiled=True)  32.7 us
    dot_general x2, matrix products, on_device(): jnp.dot(spec_rows, wave_table, preferred_element_type=jnp.float32)  13.1 us
    all_to_all x2, starting transfers between devices, on_device(): lax.all_to_all(spectrum, 'freq', split_axis=0, concat_axis=0, tiled=True)  11.9 us
    all_to_all x2, starting transfers between devices, on_device(): lax.all_to_all(piece, 'freq', split_axis=0, concat_axis=0, tiled=True)  11.6 us
    neg x1, other arithmetic, make_wave_table(): return jnp.stack([cos, -sin]).reshape(2 * F, wave_len)  9.39 us
    convert_element_type x1, other arithmetic, make_wave_table(): cos = (high_cos * low_cos - high_sin * low_sin).astype(jnp.bfloat16)  9.37 us
    another operation x1, other arithmetic, make_wave_table(): return jnp.stack([cos, -sin]).reshape(2 * F, wave_len)  6.26 us
  transfers between devices with their start and end apart: 5, of which 1 were waited for; matrix products, arithmetic and copies ran while one was open for 24% of the time, Pallas kernels for 31%

profile of v1, /device:TPU:0, one launch (start us, length us, event | category | flops | bytes accessed | tf_op | source)
XLA Modules:
  0.0 182.7 jit_solution(5593438021464321850)
XLA Ops:
  0.0 3.9 %fusion.31 = (bf16[1,1024,1,3,2,128]{5,4,3,2,1,0:T(2,128)(2,1)S(1)}, bf16[1,1024,1,3,2,128]{5,4,3,2,1,0:T(2,128)(2,1)S(1)}) fusion(bf16[1,1024,2,3,2,128]{5,4,3,2,1,0:T(2,128)(2,1)} %param.10), kind=kLoop, calls=%fused_computation.47 | loop fusion | bytes 6291456 | tf_op jit(solution)/shard_map/slice | solution.py:239
  3.9 0.0 copy-start.3
  3.9 0.2 copy.48
  4.1 1.3 copy.39
  5.4 7.3 %all-to-all-start = ((bf16[8,1,1,3,2,128,128]{6,5,4,3,2,1,0:T(8,128)(2,1)}), bf16[8,1,1,3,2,128,128]{6,5,4,3,2,1,0:T(8,128)(2,1)}, u32[]{:S(2)}, u32[]{:S(2)}) async-start(bf16[8,1,1,3,2,128,128]{6,5,4,3,2,1,0:T(8,128)(2,1)} %copy.39), calls=%async_computation | async-start | bytes 3145728 | tf_op jit(solution)/shard_map/all_to_all | solution.py:243
  12.7 0.1 collective-permute-start
  12.8 0.3 fusion.28
  13.1 0.2 copy.42
  13.3 0.2 copy.43
  13.5 0.2 copy.49
  13.7 1.2 copy.45
  15.0 2.1 %fusion.19 = (f32[1024,128]{1,0:T(8,128)S(1)}, f32[1024,128]{1,0:T(8,128)S(1)}) fusion(), kind=kLoop, calls=%fused_computation.26 | loop fusion | flops 1835008 | bytes 1048576 | tf_op jit(solution)/shard_map/sin | solution.py:178
  17.0 0.0 copy-start.4
  17.0 0.0 copy-start.7
  17.1 0.0 copy-start.6
  17.1 32.7 %all-to-all-done = bf16[8,1,1,3,2,128,128]{6,5,4,3,2,1,0:T(8,128)(2,1)} async-done(((bf16[8,1,1,3,2,128,128]{6,5,4,3,2,1,0:T(8,128)(2,1)}), bf16[8,1,1,3,2,128,128]{6,5,4,3,2,1,0:T(8,128)(2,1)}, u32[]{:S(2)}, u32[]{:S(2)}) %all-to-all-start) | async-done | bytes 1572896 | tf_op jit(solution)/shard_map/all_to_all | solution.py:243
  49.8 4.3 %all-to-all-start.2 = ((bf16[8,1,1,3,2,128,128]{6,5,4,3,2,1,0:T(8,128)(2,1)}), bf16[8,1,1,3,2,128,128]{6,5,4,3,2,1,0:T(8,128)(2,1)}, u32[]{:S(2)}, u32[]{:S(2)}) async-start(bf16[8,1,1,3,2,128,128]{6,5,4,3,2,1,0:T(8,128)(2,1)} %copy.45), calls=%async_computation.2 | async-start | bytes 3145728 | tf_op jit(solution)/shard_map/all_to_all | solution.py:243
  54.1 0.0 copy-start.5
  54.1 9.4 %fusion.6 = bf16[1,1024,16,128]{3,2,1,0:T(8,128)(2,1)} fusion(f32[1024,128]{1,0:T(8,128)S(1)} %get-tuple-element.9, f32[1024,16]{1,0:T(8,128)S(1)} %copy.43, f32[1024,128]{1,0:T(8,128)S(1)} %get-tuple-element.10, f32[1024,16]{1,0:T(8,128)S(1)} %copy.42), kind=kLoop, calls=%fused_computation.10 | loop fusion | flops 10485760 | bytes 5373952 | tf_op jit(solution)/shard_map/neg | solution.py:186
  63.5 0.1 copy.36
  63.6 0.7 reshape.219.centers
  64.3 0.1 copy.37
  64.4 0.7 reshape.220.slows
  65.1 0.6 reshape.217.lists
  65.7 0.0 collective-permute-done
  65.7 0.6 gather_fusion
  66.3 0.8 copy.40
  67.1 0.7 broadcast_in_dim.2.rise
  67.8 28.2 %shard_map.100 = bf16[8,1,3,2,64,128]{5,4,3,2,1,0:T(8,128)(2,1)} custom-call(s32[64]{0:T(128)} %reshape.217.lists, s32[8]{0:T(128)} %counts.3, s32[8]{0:T(128)} %var_counts.3, s32[8]{0:T(128)} %regions.3, s32[1]{0:T(128)} %bitcast.first_bin, f32[96]{0:T(128)} %reshape.219.centers, f32[32]{0:T(128)} %reshape.220.slows, ...), custom_call_target="tpu_custom_call" | custom-call | flops 20000000000 | bytes 40000000 | tf_op jit(solution)/shard_map/pallas_call | solution.py:140
  96.0 0.0 all-to-all-done.2
  96.0 5.9 %all-to-all-start.1 = ((bf16[8,1,3,2,64,128]{5,4,3,2,1,0:T(8,128)(2,1)}), bf16[8,1,3,2,64,128]{5,4,3,2,1,0:T(8,128)(2,1)S(1)}, u32[]{:S(2)}, u32[]{:S(2)}) async-start(bf16[8,1,3,2,64,128]{5,4,3,2,1,0:T(8,128)(2,1)} %shard_map.100), calls=%async_computation.1 | async-start | bytes 1572864 | tf_op jit(solution)/shard_map/all_to_all | solution.py:246
  101.9 28.1 %shard_map.101 = bf16[8,1,3,2,64,128]{5,4,3,2,1,0:T(8,128)(2,1)} custom-call(s32[64]{0:T(128)} %reshape.217.lists, s32[8]{0:T(128)} %counts.3, s32[8]{0:T(128)} %var_counts.3, s32[8]{0:T(128)} %regions.3, s32[1]{0:T(128)} %bitcast.first_bin, f32[96]{0:T(128)} %reshape.219.centers, f32[32]{0:T(128)} %reshape.220.slows, ...), custom_call_target="tpu_custom_call" | custom-call | flops 20000000000 | bytes 40000000 | tf_op jit(solution)/shard_map/pallas_call | solution.py:140
  130.0 0.0 all-to-all-done.1
  130.0 0.9 copy-done.1
  130.9 6.0 %all-to-all-start.3 = ((bf16[8,1,3,2,64,128]{5,4,3,2,1,0:T(8,128)(2,1)}), bf16[8,1,3,2,64,128]{5,4,3,2,1,0:T(8,128)(2,1)}, u32[]{:S(2)}, u32[]{:S(2)}) async-start(bf16[8,1,3,2,64,128]{5,4,3,2,1,0:T(8,128)(2,1)} %shard_map.101), calls=%async_computation.3 | async-start | bytes 1572864 | tf_op jit(solution)/shard_map/all_to_all | solution.py:246
  136.9 9.4 %subtract_convert_fusion = bf16[1,1024,16,128]{3,2,1,0:T(8,128)(2,1)} fusion(f32[1024,128]{1,0:T(8,128)S(1)} %get-tuple-element.9, f32[1024,16]{1,0:T(8,128)S(1)} %copy.43, f32[1024,128]{1,0:T(8,128)S(1)} %get-tuple-element.10, f32[1024,16]{1,0:T(8,128)S(1)} %copy.42), kind=kLoop, calls=%fused_computation.7 | loop fusion | flops 8388608 | bytes 5373952 | tf_op jit(solution)/shard_map/convert_element_type | solution.py:184
  146.3 6.3 %pad_maximum_fusion = bf16[2,1024,16,128]{3,2,1,0:T(8,128)(2,1)} fusion(bf16[1,1024,16,128]{3,2,1,0:T(8,128)(2,1)S(1)} %copy-done, bf16[1,1024,16,128]{3,2,1,0:T(8,128)(2,1)} %subtract_convert_fusion), kind=kLoop, calls=%fused_computation.5 | loop fusion | flops 4194304 | bytes 16777216 | tf_op jit(solution)/shard_map/stack | solution.py:186
  152.6 0.5 copy.66
  153.1 0.3 reshape.226
  153.4 6.4 %fusion.7 = f32[192,2048]{1,0:T(8,128)} fusion(bf16[192,2048]{1,0:T(8,128)(2,1)S(1)} %reshape.226, bf16[256,8,16,128]{3,2,1,0:T(8,128)(2,1)} %bitcast.43), kind=kOutput, calls=%fused_computation.12 | convolution fusion | flops 1611005952 | bytes 10747904 | tf_op jit(solution)/shard_map/dot_general | solution.py:252
  159.8 2.5 %reshape.228 = f32[64,1,3,2048]{3,2,0,1:T(4,128)S(1)} reshape(f32[192,2048]{1,0:T(8,128)} %fusion.7) | data formatting | bytes 3145728 | tf_op jit(solution)/shard_map/reshape | solution.py:255
  162.3 0.0 all-to-all-done.3
  162.3 1.6 copy.65
  164.0 1.2 reshape.232
  165.2 6.7 %fusion.10 = f32[192,2048]{1,0:T(8,128)} fusion(bf16[192,2048]{1,0:T(8,128)(2,1)} %reshape.232, bf16[256,8,16,128]{3,2,1,0:T(8,128)(2,1)} %bitcast.44), kind=kOutput, calls=%fused_computation.13 | convolution fusion | flops 1611005952 | bytes 10747904 | tf_op jit(solution)/shard_map/dot_general | solution.py:252
  171.9 3.6 %reshape.233 = f32[64,1,3,2048]{3,2,0,1:T(4,128)} reshape(f32[192,2048]{1,0:T(8,128)} %fusion.10) | data formatting | bytes 3145728 | tf_op jit(solution)/shard_map/reshape | solution.py:255
  175.5 2.7 %pad_maximum_fusion.1 = f32[64,2,3,2048]{3,2,0,1:T(4,128)S(1)} fusion(f32[64,1,3,2048]{3,2,0,1:T(4,128)} %reshape.233, f32[64,1,3,2048]{3,2,0,1:T(4,128)S(1)} %reshape.228), kind=kLoop, calls=%fused_computation.11 | loop fusion | flops 786432 | bytes 6291456 | tf_op jit(solution)/shard_map/concatenate | solution.py:256
  178.2 4.5 %copy.47 = f32[64,2,3,2048]{3,1,2,0:T(2,128)} copy(f32[64,2,3,2048]{3,2,0,1:T(4,128)S(1)} %pad_maximum_fusion.1) | data formatting | bytes 6291456 | tf_op jit(solution)/shard_map/concatenate | solution.py:256
  (14 shorter events, 0.1 us)
Async XLA Ops:
  3.9 8.8 %copy-start.3 = (bf16[8,8,8,128]{3,2,1,0:T(8,128)(2,1)S(1)}, bf16[8,8,8,128]{3,2,1,0:T(8,128)(2,1)}, u32[]{:S(2)}) copy-start(bf16[8,8,8,128]{3,2,1,0:T(8,128)(2,1)} %param.11) | copy-start | bytes 393220
  5.4 44.4 %all-to-all-start = ((bf16[8,1,1,3,2,128,128]{6,5,4,3,2,1,0:T(8,128)(2,1)}), bf16[8,1,1,3,2,128,128]{6,5,4,3,2,1,0:T(8,128)(2,1)}, u32[]{:S(2)}, u32[]{:S(2)}) async-start(bf16[8,1,1,3,2,128,128]{6,5,4,3,2,1,0:T(8,128)(2,1)} %copy.39), calls=%async_computation | async-start | bytes 3145728 | tf_op jit(solution)/shard_map/all_to_all | solution.py:243
  12.7 53.0 %collective-permute-start = (bf16[8,8,8,128]{3,2,1,0:T(8,128)(2,1)S(1)}, bf16[8,8,8,128]{3,2,1,0:T(8,128)(2,1)S(1)}, u32[]{:S(2)}, u32[]{:S(2)}) collective-permute-start(bf16[8,8,8,128]{3,2,1,0:T(8,128)(2,1)S(1)} %copy-done.3), channel_id=1, source_target_pairs={{0,1},{1,0},{2,3},{3,2},{4,5},{5,4},{6,7},{7,6},{8,9},{9,8},{10,11... | collective-permute-start | bytes 393224 | tf_op jit(solution)/shard_map/ppermute | solution.py:212
  17.0 46.5 %copy-start.4 = (f32[8,4,3]{0,1,2:T(4,128)S(1)}, f32[8,4,3]{0,1,2:T(4,128)}, u32[]{:S(2)}) copy-start(f32[8,4,3]{0,1,2:T(4,128)} %param.13) | copy-start | bytes 1156
  17.0 47.3 %copy-start.7 = (f32[8,4]{0,1:T(4,128)S(1)}, f32[8,4]{0,1:T(4,128)}, u32[]{:S(2)}) copy-start(f32[8,4]{0,1:T(4,128)} %param.14) | copy-start | bytes 388
  17.1 48.0 %copy-start.6 = (s32[8,8]{1,0:T(8,128)S(1)}, s32[8,8]{1,0:T(8,128)}, u32[]{:S(2)}) copy-start(s32[8,8]{1,0:T(8,128)} %param.16) | copy-start | bytes 772
  49.8 46.2 %all-to-all-start.2 = ((bf16[8,1,1,3,2,128,128]{6,5,4,3,2,1,0:T(8,128)(2,1)}), bf16[8,1,1,3,2,128,128]{6,5,4,3,2,1,0:T(8,128)(2,1)}, u32[]{:S(2)}, u32[]{:S(2)}) async-start(bf16[8,1,1,3,2,128,128]{6,5,4,3,2,1,0:T(8,128)(2,1)} %copy.45), calls=%async_computation.2 | async-start | bytes 3145728 | tf_op jit(solution)/shard_map/all_to_all | solution.py:243
  54.1 13.0 %copy-start.5 = (f32[8,16]{1,0:T(8,128)S(1)}, f32[8,16]{1,0:T(8,128)}, u32[]{:S(2)}) copy-start(f32[8,16]{1,0:T(8,128)} %param.15) | copy-start | bytes 1540
  96.0 34.0 %all-to-all-start.1 = ((bf16[8,1,3,2,64,128]{5,4,3,2,1,0:T(8,128)(2,1)}), bf16[8,1,3,2,64,128]{5,4,3,2,1,0:T(8,128)(2,1)S(1)}, u32[]{:S(2)}, u32[]{:S(2)}) async-start(bf16[8,1,3,2,64,128]{5,4,3,2,1,0:T(8,128)(2,1)} %shard_map.100), calls=%async_computation.1 | async-start | bytes 1572864 | tf_op jit(solution)/shard_map/all_to_all | solution.py:246
  130.0 0.9 copy-start.1
  130.9 31.4 %all-to-all-start.3 = ((bf16[8,1,3,2,64,128]{5,4,3,2,1,0:T(8,128)(2,1)}), bf16[8,1,3,2,64,128]{5,4,3,2,1,0:T(8,128)(2,1)}, u32[]{:S(2)}, u32[]{:S(2)}) async-start(bf16[8,1,3,2,64,128]{5,4,3,2,1,0:T(8,128)(2,1)} %shard_map.101), calls=%async_computation.3 | async-start | bytes 1572864 | tf_op jit(solution)/shard_map/all_to_all | solution.py:246
  136.9 9.4 %copy-start = (bf16[1,1024,16,128]{3,2,1,0:T(8,128)(2,1)S(1)}, bf16[1,1024,16,128]{3,2,1,0:T(8,128)(2,1)}, u32[]{:S(2)}) copy-start(bf16[1,1024,16,128]{3,2,1,0:T(8,128)(2,1)} %fusion.6) | copy-start | bytes 12582916
  146.3 6.3 %copy-start.2 = (bf16[8,1,3,2,64,128]{5,4,3,2,1,0:T(8,128)(2,1)S(1)}, bf16[8,1,3,2,64,128]{5,4,3,2,1,0:T(8,128)(2,1)}, u32[]{:S(2)}) copy-start(bf16[8,1,3,2,64,128]{5,4,3,2,1,0:T(8,128)(2,1)} %copy-done.1) | copy-start | bytes 2359300

commit v2 on v1

--- a/solution.py
+++ b/solution.py
@@ -6,6 +6,7 @@
 from jax.experimental import pallas as pl
 from jax.experimental.pallas import tpu as pltpu
 from jax.sharding import PartitionSpec as P
+
 
 F = 1024
 C = 3
@@ -32,36 +33,15 @@
     return 1.0 - 2.0 * half_sin * half_sin, 2.0 * half_sin * half_cos
 
 
-def synth_kernel(
-    lists,
-    counts,
-    var_counts,
-    regions,
-    first_bin,
-    centers,
-    slows,
-    tiles,
-    slip,
-    points,
-    rise,
-    out,
-    cos_buf,
-    sin_buf,
-    total,
-):
+def wave_kernel(lists, counts, first_bin, centers, slows, points, cos_out, sin_out):
     rup = pl.program_id(0)
-    sites, bins = tiles.shape[1], tiles.shape[4]
-    real_count = slip.shape[1]
-    list_len = slip.shape[0] // pl.num_programs(0)
-    hypo_count = cos_buf.shape[0] * 2
+    _, list_len, pairs, bins, _ = cos_out.shape
+    hypo_count = pairs * 2
     step = 16
     start = first_bin[0]
-    total[...] = jnp.zeros_like(total)
 
     def one_slot(place, carry):
-        block = lists[rup * list_len + place]
-        region = regions[block]
-        xyz = points[block]
+        xyz = points[lists[rup * list_len + place]]
         low = lax.broadcasted_iota(jnp.int32, (step, LANES), 0).astype(jnp.float32)
         high = (start + step * lax.broadcasted_iota(jnp.int32, (bins // step, LANES), 0)).astype(
             jnp.float32
@@ -81,10 +61,47 @@
                 hc, hs = high_cos[part : part + 1], high_sin[part : part + 1]
                 cos = (hc * low_cos - hs * low_sin).astype(jnp.bfloat16)
                 sin = (hs * low_cos + hc * low_sin).astype(jnp.bfloat16)
-                rows = pl.ds(part * step, step)
-                cos_buf[hypo // 2, rows, lane : lane + LANES] = cos
-                sin_buf[hypo // 2, rows, lane : lane + LANES] = sin
-        amps = slip[rup * list_len + place]
+                rows = slice(part * step, (part + 1) * step)
+                cos_out[0, place, hypo // 2, rows, lane : lane + LANES] = cos
+                sin_out[0, place, hypo // 2, rows, lane : lane + LANES] = sin
+        return carry
+
+    lax.fori_loop(0, counts[rup], one_slot, 0)
+
+
+def make_waves(points, scalars, rupture_count, list_len, hypo_count, bins):
+    block = (1, list_len, hypo_count // 2, bins, 2 * LANES)
+    shape = jax.ShapeDtypeStruct((rupture_count,) + block[1:], jnp.bfloat16)
+    spec = pl.BlockSpec(block, lambda r, *_: (r, 0, 0, 0, 0))
+    return pl.pallas_call(
+        wave_kernel,
+        grid_spec=pltpu.PrefetchScalarGridSpec(
+            num_scalar_prefetch=len(scalars),
+            grid=(rupture_count,),
+            in_specs=[pl.BlockSpec(memory_space=pltpu.VMEM)],
+            out_specs=[spec, spec],
+        ),
+        out_shape=[shape, shape],
+        compiler_params=pltpu.CompilerParams(dimension_semantics=("arbitrary",)),
+        cost_estimate=pl.CostEstimate(flops=10**6, bytes_accessed=10**5, transcendentals=0),
+    )(*scalars, points)
+
+
+def synth_kernel(
+    lists, counts, var_counts, regions, first_bin, tiles, slip, cos_in, sin_in, rise, out, total
+):
+    rup = pl.program_id(0)
+    sites, bins = tiles.shape[1], tiles.shape[4]
+    _, list_len, pairs, _, _ = cos_in.shape
+    real_count = slip.shape[1]
+    hypo_count = pairs * 2
+    start = first_bin[0]
+    total[...] = jnp.zeros_like(total)
+
+    def one_slot(place, carry):
+        slot = rup * list_len + place
+        region = regions[lists[slot]]
+        amps = slip[slot]
         none = jnp.zeros_like(amps)
         paired = jnp.concatenate(
             [jnp.concatenate([amps, none], axis=1), jnp.concatenate([none, amps], axis=1)], axis=0
@@ -95,8 +112,8 @@
                 tile_im = tiles[region, site, comp, 1]
                 tile_re = jnp.concatenate([tile_re, tile_re], axis=1)
                 tile_im = jnp.concatenate([tile_im, tile_im], axis=1)
-                for pair in range(hypo_count // 2):
-                    cos, sin = cos_buf[pair], sin_buf[pair]
+                for pair in range(pairs):
+                    cos, sin = cos_in[0, place, pair], sin_in[0, place, pair]
                     weighted = jnp.concatenate(
                         [cos * tile_re + sin * tile_im, cos * tile_im - sin * tile_re], axis=0
                     )
@@ -132,10 +149,12 @@
                     out[0, site, comp, 1, kept] = jnp.where(live, spec_im, 0.0).astype(out.dtype)
 
 
-def synthesize(tiles, slip, points, rise, scalars, hypo_count):
-    rupture_count = rise.shape[0]
-    real_count = rise.shape[1]
+def synthesize(tiles, slip, cos_waves, sin_waves, rise, scalars):
+    rupture_count, real_count, _ = rise.shape
     _, sites, _, _, bins, _ = tiles.shape
+    pairs = cos_waves.shape[2]
+    rows = 2 * pairs * real_count
+    wave_spec = pl.BlockSpec((1,) + cos_waves.shape[1:], lambda r, *_: (r, 0, 0, 0, 0))
     whole = pl.BlockSpec(memory_space=pltpu.VMEM)
     return pl.pallas_call(
         synth_kernel,
@@ -145,45 +164,125 @@
             in_specs=[
                 whole,
                 whole,
-                whole,
+                wave_spec,
+                wave_spec,
                 pl.BlockSpec((1, real_count, bins), lambda r, *_: (r, 0, 0)),
             ],
             out_specs=pl.BlockSpec(
-                (1, sites, C, 2, hypo_count * real_count, bins),
-                lambda r, *_: (r, 0, 0, 0, 0, 0),
+                (1, sites, C, 2, rows, bins), lambda r, *_: (r, 0, 0, 0, 0, 0)
             ),
-            scratch_shapes=[
-                pltpu.VMEM((hypo_count // 2, bins, 2 * LANES), jnp.bfloat16),
-                pltpu.VMEM((hypo_count // 2, bins, 2 * LANES), jnp.bfloat16),
-                pltpu.VMEM((sites, C, hypo_count // 2, 2 * real_count, 2 * bins), jnp.float32),
-            ],
+            scratch_shapes=[pltpu.VMEM((sites, C, pairs, 2 * real_count, 2 * bins), jnp.float32)],
         ),
-        out_shape=jax.ShapeDtypeStruct(
-            (rupture_count, sites, C, 2, hypo_count * real_count, bins), jnp.bfloat16
-        ),
+        out_shape=jax.ShapeDtypeStruct((rupture_count, sites, C, 2, rows, bins), jnp.bfloat16),
         compiler_params=pltpu.CompilerParams(dimension_semantics=("arbitrary",)),
         cost_estimate=pl.CostEstimate(
             flops=sites * 2 * 10**10, bytes_accessed=4 * 10**7, transcendentals=0
         ),
-    )(*scalars, tiles, slip, points, rise)
+    )(*scalars, tiles, slip, cos_waves, sin_waves, rise)
+
+
+def table_kernel(out):
+    rows, wave_len = out.shape[1:]
+    period = wave_len // LANES
+    first = pl.program_id(0) * rows
+    bins = first + lax.broadcasted_iota(jnp.int32, (rows, LANES), 0)
+    samples = lax.broadcasted_iota(jnp.int32, (rows, LANES), 1)
+    turns = (bins * samples % wave_len).astype(jnp.float32) * (1.0 / wave_len)
+    low_cos, low_sin = turn_waves(turns)
+    residues = first + lax.broadcasted_iota(jnp.int32, (period, LANES), 0)
+    for chunk in range(period):
+        turns = (residues * chunk % period).astype(jnp.float32) * (1.0 / period)
+        high_cos, high_sin = turn_waves(turns)
+        lanes = slice(chunk * LANES, (chunk + 1) * LANES)
+        for part in range(rows // period):
+            here = slice(part * period, (part + 1) * period)
+            lc, ls = low_cos[here], low_sin[here]
+            out[0, here, lanes] = (high_cos * lc - high_sin * ls).astype(out.dtype)
+            out[1, here, lanes] = (-(high_sin * lc + high_cos * ls)).astype(out.dtype)
 
 
 def make_wave_table():
     wave_len = 2 * F
-    chunk = LANES
-    bins = jnp.arange(F, dtype=jnp.int32)[:, None]
-
-    def waves(samples):
-        angles = TWO_PI / wave_len * (bins * samples[None, :] % wave_len).astype(jnp.float32)
-        return jnp.cos(angles), jnp.sin(angles)
-
-    low_cos, low_sin = waves(jnp.arange(chunk, dtype=jnp.int32))
-    high_cos, high_sin = waves(jnp.arange(wave_len // chunk, dtype=jnp.int32) * chunk)
-    low_cos, low_sin = low_cos[:, None, :], low_sin[:, None, :]
-    high_cos, high_sin = high_cos[:, :, None], high_sin[:, :, None]
-    cos = (high_cos * low_cos - high_sin * low_sin).astype(jnp.bfloat16)
-    sin = (high_sin * low_cos + high_cos * low_sin).astype(jnp.bfloat16)
-    return jnp.stack([cos, -sin]).reshape(2 * F, wave_len)
+    rows = 128
+    table = pl.pallas_call(
+        table_kernel,
+        grid=(F // rows,),
+        out_specs=pl.BlockSpec((2, rows, wave_len), lambda i: (0, i, 0)),
+        out_shape=jax.ShapeDtypeStruct((2, F, wave_len), jnp.bfloat16),
+        compiler_params=pltpu.CompilerParams(dimension_semantics=("arbitrary",)),
+        cost_estimate=pl.CostEstimate(flops=10**6, bytes_accessed=10**5, transcendentals=0),
+    )()
+    return table.reshape(2 * F, wave_len)
+
+
+def rows_to_motion(spectra, table):
+    freq_count, _, comps, _, _, _ = spectra.shape
+    lines = [
+        jnp.concatenate(
+            [spectra[f, 0, comp, part] for part in range(2) for f in range(freq_count)], axis=1
+        )
+        for comp in range(comps)
+    ]
+    return jnp.dot(
+        jnp.concatenate(lines, axis=0), table[...], preferred_element_type=jnp.float32
+    ) * (OUT_GAIN / math.sqrt(F))
+
+
+def early_kernel(spectra, table, out):
+    out[...] = rows_to_motion(spectra, table)
+
+
+def last_kernel(spectra, table, *rest):
+    early, out = rest[:-1], rest[-1]
+    reals, hypos, comps, sites, _ = out.shape
+    for site in range(sites):
+        motion = early[site][...] if site < sites - 1 else rows_to_motion(spectra, table)
+        for comp in range(comps):
+            for hypo in range(hypos):
+                first = (comp * hypos + hypo) * reals
+                out[:, hypo, comp, site, :] = motion[first : first + reals]
+
+
+def early_motion(spectra, table):
+    _, _, comps, _, rows, _ = spectra.shape
+    depth, wave_len = table.shape
+    piece = 512
+    return pl.pallas_call(
+        early_kernel,
+        grid=(wave_len // piece,),
+        in_specs=[
+            pl.BlockSpec(memory_space=pltpu.VMEM),
+            pl.BlockSpec((depth, piece), lambda i: (0, i)),
+        ],
+        out_specs=pl.BlockSpec((comps * rows, piece), lambda i: (0, i)),
+        out_shape=jax.ShapeDtypeStruct((comps * rows, wave_len), jnp.float32),
+        compiler_params=pltpu.CompilerParams(dimension_semantics=("arbitrary",)),
+        cost_estimate=pl.CostEstimate(flops=10**9, bytes_accessed=10**7, transcendentals=0),
+    )(spectra, table)
+
+
+def last_motion(spectra, table, early, real_count, hypo_count):
+    _, _, comps, _, rows, _ = spectra.shape
+    depth, wave_len = table.shape
+    sites = len(early) + 1
+    piece = 512
+    return pl.pallas_call(
+        last_kernel,
+        grid=(wave_len // piece,),
+        in_specs=[
+            pl.BlockSpec(memory_space=pltpu.VMEM),
+            pl.BlockSpec((depth, piece), lambda i: (0, i)),
+        ]
+        + [pl.BlockSpec((comps * rows, piece), lambda i: (0, i)) for _ in early],
+        out_specs=pl.BlockSpec(
+            (real_count, hypo_count, comps, sites, piece), lambda i: (0, 0, 0, 0, i)
+        ),
+        out_shape=jax.ShapeDtypeStruct(
+            (real_count, hypo_count, comps, sites, wave_len), jnp.float32
+        ),
+        compiler_params=pltpu.CompilerParams(dimension_semantics=("arbitrary",)),
+        cost_estimate=pl.CostEstimate(flops=10**9, bytes_accessed=10**7, transcendentals=0),
+    )(spectra, table, *early)
 
 
 def on_device(
@@ -204,7 +303,6 @@
     point_count = green.shape[-1]
     rupture_count, list_len = block_lists.shape
     hypo_count = hypocenters.shape[1]
-    wave_len = 2 * F
     block_total = positions.shape[1] // point_count
     pieces = [slip]
     for shift in range(1, site_shards):
@@ -213,28 +311,33 @@
                 slip, "site", [(i, (i - shift) % site_shards) for i in range(site_shards)]
             )
         )
-    ring = jnp.stack(pieces)
     own = lax.axis_index("site")
-    order = (jnp.arange(site_shards) - own) % site_shards
-    slip_all = ring[order].transpose(1, 3, 0, 2, 4)
-    real_count = site_shards * slip.shape[1]
+    slots = []
+    for shard in range(site_shards):
+        piece = pieces[0]
+        for shift in range(1, site_shards):
+            piece = jnp.where((own + shift) % site_shards == shard, pieces[shift], piece)
+        slots.append(piece)
+    slip_all = jnp.concatenate(slots, axis=1).transpose(0, 2, 1, 3)
+    real_count = slip_all.shape[2]
     slip_all = slip_all.reshape(rupture_count * list_len, real_count, point_count)
     points = positions.reshape(3, block_total, point_count).transpose(1, 0, 2)
     first_bin = (lax.axis_index("freq") * fdev_bins).astype(jnp.int32).reshape(1)
-    scalars = (
-        block_lists.reshape(-1),
-        block_counts,
-        var_counts,
-        region_map,
-        first_bin,
-        hypocenters.reshape(-1),
-        slowness.reshape(-1),
+    lists = block_lists.reshape(-1)
+    rise_rows = jnp.broadcast_to(rise[:, :, None], (rupture_count, real_count, fdev_bins))
+    cos_waves, sin_waves = make_waves(
+        points,
+        (lists, block_counts, first_bin, hypocenters.reshape(-1), slowness.reshape(-1)),
+        rupture_count,
+        list_len,
+        hypo_count,
+        fdev_bins,
     )
-    rise_rows = jnp.broadcast_to(rise[:, :, None], (rupture_count, real_count, fdev_bins))
+    table = make_wave_table()
     site_items = green.shape[2]
     rows_here, _, _, comps, _, _ = green.shape
-    wave_table = make_wave_table()
-    motions = []
+    scalars = (lists, block_counts, var_counts, region_map, first_bin)
+    early = []
     for site in range(site_items):
         piece = green[:, :, site : site + 1].reshape(
             rows_here, freq_count, fdev_bins, 1, comps, 2, point_count
@@ -242,18 +345,14 @@
         piece = piece.transpose(1, 0, 3, 4, 5, 2, 6)
         tiles = lax.all_to_all(piece, "freq", split_axis=0, concat_axis=0, tiled=True)
         tiles = tiles.reshape(freq_count * rows_here, 1, comps, 2, fdev_bins, point_count)
-        spectrum = synthesize(tiles, slip_all, points, rise_rows, scalars, hypo_count)
+        spectrum = synthesize(tiles, slip_all, cos_waves, sin_waves, rise_rows, scalars)
         own_rows = lax.all_to_all(spectrum, "freq", split_axis=0, concat_axis=0, tiled=True)
-        own_rows = own_rows.reshape(
-            freq_count, rupture_count // freq_count, comps, 2, hypo_count, real_count, fdev_bins
-        ).transpose(1, 5, 4, 2, 3, 0, 6)
-        row_count = rupture_count // freq_count * hypo_count * real_count
-        spec_rows = own_rows.reshape(row_count * comps, wave_len)
-        motion = jnp.dot(spec_rows, wave_table, preferred_element_type=jnp.float32) * (
-            OUT_GAIN / math.sqrt(F)
-        )
-        motions.append(motion.reshape(row_count, 1, comps, wave_len))
-    return jnp.concatenate(motions, axis=1)
+        if site < site_items - 1:
+            early.append(early_motion(own_rows, table))
+        else:
+            motion = last_motion(own_rows, table, early, real_count, hypo_count)
+    motion = motion.reshape(real_count * hypo_count, comps, site_items, 2 * F)
+    return motion.transpose(0, 2, 1, 3)
 
 
 def on_device_small(
@@ -370,7 +469,7 @@
     fdev_bins = green.shape[1] // freq_count
     rupture_count, hypo_count = hypocenters.shape[:2]
     lanes_fit = fdev_bins == LANES and green.shape[-1] == LANES
-    if lanes_fit and hypo_count % 2 == 0 and rupture_count % freq_count == 0:
+    if lanes_fit and hypo_count % 2 == 0 and rupture_count == freq_count:
         return on_device(green, slip, positions, hypocenters, *rest)
     return on_device_small(green, slip, positions, hypocenters, *rest)
 

time: 183 us -> 156 us (0.85)
  other arithmetic: 30.1 us -> 0.05 us
  Pallas kernels: 56.3 us -> 76.7 us
  matrix products: 13.1 us -> 0 us
  local copies, waits for them, and re-layouts: 26.7 us -> 13.6 us
  waiting for transfers between devices: 32.7 us -> 42.3 us
    pallas_call x0 -> x4, Pallas kernels: none -> 32.8 us  [the longest x1 11.9 us: make_waves(): pl.pallas_call(wave_kernel, grid_spec=pltpu.PrefetchScalarGridSpec(num_sc...]
    dot_general x2 -> x0, matrix products: 13.1 us -> none  [on_device(): jnp.dot(spec_rows, wave_table, preferred_element_type=jnp.float32)]
    pallas_call x2, Pallas kernels: 56.3 us -> 44 us  [synthesize(): pl.pallas_call(synth_kernel, grid_spec=pltpu.PrefetchScalarGridSpec(num_s...]
    reshape x7 -> x1, local copies, waits for them, and re-layouts: 10.5 us -> 0.63 us  [on_device(): lists = block_lists.reshape(-1)]
    neg x1 -> x0, other arithmetic: 9.39 us -> none  [make_wave_table(): return jnp.stack([cos, -sin]).reshape(2 * F, wave_len)]
    convert_element_type x1 -> x0, other arithmetic: 9.37 us -> none  [make_wave_table(): cos = (high_cos * low_cos - high_sin * low_sin).astype(jnp.bfloat16)]
    all_to_all x2, waiting for transfers between devices: 0.01 us -> 6.75 us  [on_device(): lax.all_to_all(spectrum, 'freq', split_axis=0, concat_axis=0, tiled=True)]
    another operation x2 -> x0, other arithmetic: 6.29 us -> none  [the longest x1 6.26 us: make_wave_table(): return jnp.stack([cos, -sin]).reshape(2 * F, wave_len)]
  transfers between devices with their start and end apart: 5 -> 5, of which waited for: 1 -> 2; matrix products, arithmetic and copies ran while one was open for 24% -> 3% of each run, Pallas kernels for 31% -> 45%
where the time goes in v2:
time: 156 us
  Pallas kernels  76.7 us (49%)
  waiting for transfers between devices  42.3 us (27%)
  starting transfers between devices  23 us (15%)
  local copies, waits for them, and re-layouts  13.6 us (9%)
    pallas_call x2, Pallas kernels, synthesize(): pl.pallas_call(synth_kernel, grid_spec=pltpu.PrefetchScalarGridSpec(num_s...  44 us
    all_to_all x2, waiting for transfers between devices, on_device(): lax.all_to_all(piece, 'freq', split_axis=0, concat_axis=0, tiled=True)  35.5 us
    all_to_all x2, starting transfers between devices, on_device(): lax.all_to_all(spectrum, 'freq', split_axis=0, concat_axis=0, tiled=True)  12 us
    pallas_call x1, Pallas kernels, make_waves(): pl.pallas_call(wave_kernel, grid_spec=pltpu.PrefetchScalarGridSpec(num_sc...  11.9 us
    all_to_all x2, starting transfers between devices, on_device(): lax.all_to_all(piece, 'freq', split_axis=0, concat_axis=0, tiled=True)  10.9 us
    pallas_call x1, Pallas kernels, last_motion(): pl.pallas_call(last_kernel, grid=(wave_len // piece,), in_specs=[pl.Block...  7.37 us
    pallas_call x1, Pallas kernels, make_wave_table(): pl.pallas_call(table_kernel, grid=(F // rows,), out_specs=pl.BlockSpec((2...  7.15 us
    all_to_all x2, waiting for transfers between devices, on_device(): lax.all_to_all(spectrum, 'freq', split_axis=0, concat_axis=0, tiled=True)  6.75 us
  transfers between devices with their start and end apart: 5, of which 2 were waited for; matrix products, arithmetic and copies ran while one was open for 3% of the time, Pallas kernels for 45%

profile of v2, /device:TPU:0, one launch (start us, length us, event | category | flops | bytes accessed | tf_op | source)
XLA Modules:
  0.0 155.8 jit_solution(10339623264359777711)
XLA Ops:
  0.0 3.9 %fusion = (bf16[1,1024,1,3,2,128]{5,4,3,2,1,0:T(2,128)(2,1)S(1)}, bf16[1,1024,1,3,2,128]{5,4,3,2,1,0:T(2,128)(2,1)S(1)}) fusion(bf16[1,1024,2,3,2,128]{5,4,3,2,1,0:T(2,128)(2,1)} %param.10), kind=kLoop, calls=%fused_computation.3 | loop fusion | bytes 6291456 | tf_op jit(solution)/shard_map/slice | solution.py:342
  3.9 0.2 copy.29
  4.1 1.3 copy.27
  5.4 7.3 %all-to-all-start.2 = ((bf16[8,1,1,3,2,128,128]{6,5,4,3,2,1,0:T(8,128)(2,1)}), bf16[8,1,1,3,2,128,128]{6,5,4,3,2,1,0:T(8,128)(2,1)S(1)}, u32[]{:S(2)}, u32[]{:S(2)}) async-start(bf16[8,1,1,3,2,128,128]{6,5,4,3,2,1,0:T(8,128)(2,1)} %copy.27), calls=%async_computation.2 | async-start | bytes 3145728 | tf_op jit(solution)/shard_map/all_to_all | solution.py:346
  12.6 0.2 copy.28
  12.8 1.2 copy.22
  14.1 0.0 copy-start.4
  14.1 0.0 copy-start.7
  14.1 0.0 copy-start.8
  14.1 0.0 copy-start.5
  14.1 35.5 %all-to-all-done.2 = bf16[8,1,1,3,2,128,128]{6,5,4,3,2,1,0:T(8,128)(2,1)S(1)} async-done(((bf16[8,1,1,3,2,128,128]{6,5,4,3,2,1,0:T(8,128)(2,1)}), bf16[8,1,1,3,2,128,128]{6,5,4,3,2,1,0:T(8,128)(2,1)S(1)}, u32[]{:S(2)}, u32[]{:S(2)}) %all-to-all-start.2) | async-done | bytes 1572896 | tf_op jit(solution)/shard_map/all_to_all | solution.py:346
  49.6 0.0 copy-start.2
  49.6 1.2 copy-done.2
  50.8 3.6 %all-to-all-start = ((bf16[8,1,1,3,2,128,128]{6,5,4,3,2,1,0:T(8,128)(2,1)}), bf16[8,1,1,3,2,128,128]{6,5,4,3,2,1,0:T(8,128)(2,1)S(1)}, u32[]{:S(2)}, u32[]{:S(2)}) async-start(bf16[8,1,1,3,2,128,128]{6,5,4,3,2,1,0:T(8,128)(2,1)} %copy.22), calls=%async_computation | async-start | bytes 3145728 | tf_op jit(solution)/shard_map/all_to_all | solution.py:346
  54.5 0.0 copy-done.4
  54.5 0.0 copy-start.6
  54.5 0.1 collective-permute-start
  54.6 0.0 copy-done.7
  54.6 0.6 reshape.37.lists
  55.2 0.0 copy-done.8
  55.2 0.1 copy.25
  55.3 0.7 reshape.43.slows
  55.9 0.0 copy-done.5
  56.0 0.1 copy.24
  56.1 0.7 reshape.42.centers
  56.7 11.9 %shard_map.100 = (bf16[8,8,2,128,256]{4,3,2,1,0:T(8,128)(2,1)}, bf16[8,8,2,128,256]{4,3,2,1,0:T(8,128)(2,1)}) custom-call(s32[64]{0:T(128)} %reshape.37.lists, s32[8]{0:T(128)} %counts.5, s32[1]{0:T(128)} %bitcast.first_bin, f32[96]{0:T(128)} %reshape.42.centers, f32[32]{0:T(128)} %reshape.43.slows, f32[8,3,128]{2,1,0:T(4,128)} %bitcast.27), custom_call_target="tpu_custom_call" | custom-call | flops 1000000 | bytes 100000 | tf_op jit(solution)/shard_map/pallas_call | solution.py:76
  68.6 0.0 collective-permute-done
  68.7 0.8 copy.23
  69.4 0.0 copy-done.6
  69.4 0.7 broadcast_in_dim.2.rise
  70.1 22.0 %shard_map.103 = bf16[8,1,3,2,64,128]{5,4,3,2,1,0:T(8,128)(2,1)} custom-call(s32[64]{0:T(128)} %reshape.37.lists, s32[8]{0:T(128)} %counts.5, s32[8]{0:T(128)} %var_counts.3, s32[8]{0:T(128)} %regions.3, s32[1]{0:T(128)} %bitcast.first_bin, bf16[8,1,3,2,128,128]{5,4,3,2,1,0:T(8,128)(2,1)} %bitcast.23, bf16[64,16,128]{2,1,0:T(8,128)(2,1)} %bitcast.25, ...), custom_call_target="tpu_custom_call" | custom-call | flops 20000000000 | bytes 40000000 | tf_op jit(solution)/shard_map/pallas_call | solution.py:159
  92.1 0.0 all-to-all-done
  92.1 0.0 copy-start.3
  92.1 1.1 copy-done.3
  93.3 6.0 %all-to-all-start.3 = ((bf16[8,1,3,2,64,128]{5,4,3,2,1,0:T(8,128)(2,1)}), bf16[8,1,3,2,64,128]{5,4,3,2,1,0:T(8,128)(2,1)S(1)}, u32[]{:S(2)}, u32[]{:S(2)}) async-start(bf16[8,1,3,2,64,128]{5,4,3,2,1,0:T(8,128)(2,1)} %shard_map.103), calls=%async_computation.3 | async-start | bytes 1572864 | tf_op jit(solution)/shard_map/all_to_all | solution.py:349
  99.2 22.0 %shard_map.101 = bf16[8,1,3,2,64,128]{5,4,3,2,1,0:T(8,128)(2,1)} custom-call(s32[64]{0:T(128)} %reshape.37.lists, s32[8]{0:T(128)} %counts.5, s32[8]{0:T(128)} %var_counts.3, s32[8]{0:T(128)} %regions.3, s32[1]{0:T(128)} %bitcast.first_bin, bf16[8,1,3,2,128,128]{5,4,3,2,1,0:T(8,128)(2,1)} %bitcast.24, bf16[64,16,128]{2,1,0:T(8,128)(2,1)} %bitcast.26, ...), custom_call_target="tpu_custom_call" | custom-call | flops 20000000000 | bytes 40000000 | tf_op jit(solution)/shard_map/pallas_call | solution.py:159
  121.2 0.0 all-to-all-done.3.spectra
  121.2 0.0 copy-start
  121.3 6.0 %all-to-all-start.1 = ((bf16[8,1,3,2,64,128]{5,4,3,2,1,0:T(8,128)(2,1)}), bf16[8,1,3,2,64,128]{5,4,3,2,1,0:T(8,128)(2,1)S(1)}, u32[]{:S(2)}, u32[]{:S(2)}) async-start(bf16[8,1,3,2,64,128]{5,4,3,2,1,0:T(8,128)(2,1)} %shard_map.101), calls=%async_computation.1 | async-start | bytes 1572864 | tf_op jit(solution)/shard_map/all_to_all | solution.py:349
  127.3 7.2 %shard_map.102 = bf16[2,1024,2048]{2,1,0:T(8,128)(2,1)} custom-call(), custom_call_target="tpu_custom_call" | custom-call | flops 1000000 | bytes 100000 | tf_op jit(solution)/shard_map/pallas_call | solution.py:207
  134.4 0.0 copy-done
  134.4 6.4 %shard_map.104.rest_0_ = f32[192,2048]{1,0:T(8,128)} custom-call(bf16[8,1,3,2,64,128]{5,4,3,2,1,0:T(8,128)(2,1)} %copy-done, bf16[2048,2048]{1,0:T(8,128)(2,1)} %bitcast.19), custom_call_target="tpu_custom_call" | custom-call | flops 1000000000 | bytes 10000000 | tf_op jit(solution)/shard_map/pallas_call | solution.py:250
  140.8 6.7 %all-to-all-done.1.spectra = bf16[8,1,3,2,64,128]{5,4,3,2,1,0:T(8,128)(2,1)S(1)} async-done(((bf16[8,1,3,2,64,128]{5,4,3,2,1,0:T(8,128)(2,1)}), bf16[8,1,3,2,64,128]{5,4,3,2,1,0:T(8,128)(2,1)S(1)}, u32[]{:S(2)}, u32[]{:S(2)}) %all-to-all-start.1) | async-done | bytes 786464 | tf_op jit(solution)/shard_map/all_to_all | solution.py:349
  147.5 0.0 copy-start.1
  147.5 0.9 copy-done.1
  148.4 7.4 %shard_map.105 = f32[16,4,3,2,2048]{4,3,2,1,0:T(2,128)} custom-call(bf16[8,1,3,2,64,128]{5,4,3,2,1,0:T(8,128)(2,1)} %copy-done.1, bf16[2048,2048]{1,0:T(8,128)(2,1)} %bitcast.20, f32[192,2048]{1,0:T(8,128)} %shard_map.104.rest_0_), custom_call_target="tpu_custom_call" | custom-call | flops 1000000000 | bytes 10000000 | tf_op jit(solution)/shard_map/pallas_call | solution.py:269
  (2 shorter events, 0.0 us)
Async XLA Ops:
  5.4 44.3 %all-to-all-start.2 = ((bf16[8,1,1,3,2,128,128]{6,5,4,3,2,1,0:T(8,128)(2,1)}), bf16[8,1,1,3,2,128,128]{6,5,4,3,2,1,0:T(8,128)(2,1)S(1)}, u32[]{:S(2)}, u32[]{:S(2)}) async-start(bf16[8,1,1,3,2,128,128]{6,5,4,3,2,1,0:T(8,128)(2,1)} %copy.27), calls=%async_computation.2 | async-start | bytes 3145728 | tf_op jit(solution)/shard_map/all_to_all | solution.py:346
  14.1 40.4 %copy-start.4 = (bf16[8,8,8,128]{3,2,1,0:T(8,128)(2,1)S(1)}, bf16[8,8,8,128]{3,2,1,0:T(8,128)(2,1)}, u32[]{:S(2)}) copy-start(bf16[8,8,8,128]{3,2,1,0:T(8,128)(2,1)} %param.11) | copy-start | bytes 393220
  14.1 40.5 %copy-start.7 = (s32[8,8]{1,0:T(8,128)S(1)}, s32[8,8]{1,0:T(8,128)}, u32[]{:S(2)}) copy-start(s32[8,8]{1,0:T(8,128)} %param.16) | copy-start | bytes 772
  14.1 41.1 %copy-start.8 = (f32[8,4]{0,1:T(4,128)S(1)}, f32[8,4]{0,1:T(4,128)}, u32[]{:S(2)}) copy-start(f32[8,4]{0,1:T(4,128)} %param.14) | copy-start | bytes 388
  14.1 41.8 %copy-start.5 = (f32[8,4,3]{0,1,2:T(4,128)S(1)}, f32[8,4,3]{0,1,2:T(4,128)}, u32[]{:S(2)}) copy-start(f32[8,4,3]{0,1,2:T(4,128)} %param.13) | copy-start | bytes 1156
  49.6 1.2 copy-start.2
  50.8 41.3 %all-to-all-start = ((bf16[8,1,1,3,2,128,128]{6,5,4,3,2,1,0:T(8,128)(2,1)}), bf16[8,1,1,3,2,128,128]{6,5,4,3,2,1,0:T(8,128)(2,1)S(1)}, u32[]{:S(2)}, u32[]{:S(2)}) async-start(bf16[8,1,1,3,2,128,128]{6,5,4,3,2,1,0:T(8,128)(2,1)} %copy.22), calls=%async_computation | async-start | bytes 3145728 | tf_op jit(solution)/shard_map/all_to_all | solution.py:346
  54.5 15.0 %copy-start.6 = (f32[8,16]{1,0:T(8,128)S(1)}, f32[8,16]{1,0:T(8,128)}, u32[]{:S(2)}) copy-start(f32[8,16]{1,0:T(8,128)} %param.15) | copy-start | bytes 1540
  54.5 14.1 %collective-permute-start = (bf16[8,8,8,128]{3,2,1,0:T(8,128)(2,1)S(1)}, bf16[8,8,8,128]{3,2,1,0:T(8,128)(2,1)S(1)}, u32[]{:S(2)}, u32[]{:S(2)}) collective-permute-start(bf16[8,8,8,128]{3,2,1,0:T(8,128)(2,1)S(1)} %copy-done.4), channel_id=1, source_target_pairs={{0,1},{1,0},{2,3},{3,2},{4,5},{5,4},{6,7},{7,6},{8,9},{9,8},{10,11... | collective-permute-start | bytes 393224 | tf_op jit(solution)/shard_map/ppermute | solution.py:310
  92.1 1.1 copy-start.3
  93.3 28.0 %all-to-all-start.3 = ((bf16[8,1,3,2,64,128]{5,4,3,2,1,0:T(8,128)(2,1)}), bf16[8,1,3,2,64,128]{5,4,3,2,1,0:T(8,128)(2,1)S(1)}, u32[]{:S(2)}, u32[]{:S(2)}) async-start(bf16[8,1,3,2,64,128]{5,4,3,2,1,0:T(8,128)(2,1)} %shard_map.103), calls=%async_computation.3 | async-start | bytes 1572864 | tf_op jit(solution)/shard_map/all_to_all | solution.py:349
  121.2 13.2 %copy-start = (bf16[8,1,3,2,64,128]{5,4,3,2,1,0:T(8,128)(2,1)}, bf16[8,1,3,2,64,128]{5,4,3,2,1,0:T(8,128)(2,1)S(1)}, u32[]{:S(2)}) copy-start(bf16[8,1,3,2,64,128]{5,4,3,2,1,0:T(8,128)(2,1)S(1)} %all-to-all-done.3.spectra) | copy-start | bytes 2359300
  121.3 26.3 %all-to-all-start.1 = ((bf16[8,1,3,2,64,128]{5,4,3,2,1,0:T(8,128)(2,1)}), bf16[8,1,3,2,64,128]{5,4,3,2,1,0:T(8,128)(2,1)S(1)}, u32[]{:S(2)}, u32[]{:S(2)}) async-start(bf16[8,1,3,2,64,128]{5,4,3,2,1,0:T(8,128)(2,1)} %shard_map.101), calls=%async_computation.1 | async-start | bytes 1572864 | tf_op jit(solution)/shard_map/all_to_all | solution.py:349
  147.5 0.9 copy-start.1
